TPU v7x, 256 devices: a whole 4x4x8 slice. The times are simulated.
256 devices in a mesh: au: 32 (over y, x, core), ia: 8 (over z).
Axes of the slice: x: 4, y: 4, z: 8, core: 2. Of those that a mesh axis runs over, the one named last changes fastest.
Arguments:
- user_emb: float32 [131072, 128], P(('au', 'ia')), may hold values from -6 to 6
- item_emb: float32 [32768, 128], P(('ia', 'au')), may hold values from -6 to 6
- user_degree: int32 [131072], P(('au', 'ia')), may hold values from 1 to 64
- item_degree: int32 [32768], P(('ia', 'au')), may hold values from 1 to 64
- tiles: float32 [32768, 128, 128], P(('au', 'ia')), as said below
- tile_user_block: int32 [32768], P(('au', 'ia')), may hold values from 0 to 31
- tile_item_block: int32 [32768], P(('au', 'ia')), may hold values from 0 to 31
- live_tiles: int32 [256], P(('au', 'ia')), may hold values from 32 to 128, as said below
Outputs:
- user_final: float32 [131072, 128], P(('au', 'ia'))
- item_final: float32 [32768, 128], P(('ia', 'au'))
Inputs may be any that keep to these rules, and one draw needn't show every extreme that they name: Tile slots of grid cell c beyond the first live_tiles[c] are unused; some cell uses all 128. `tiles`: each tile holds weights of 0 or between 0.05 and 0.35.
All inputs are finite; a program needn't handle non-finite values.
Results may differ from a plain program's by a relative error of at most 0.0001.
Values sent between devices are 32-bit elements; how exact they have to be, the bound alone decides.
A program may use at most 128 MiB of HBM per device.

v0:
```python
import jax
import jax.numpy as jnp
from jax import lax
from jax.sharding import PartitionSpec as P

LAYERS = 2


def per_device(
    user_emb,
    item_emb,
    user_degree,
    item_degree,
    tiles,
    tile_user_block,
    tile_item_block,
    live_tiles,
):
    tile_size = tiles.shape[1]
    emb_width = user_emb.shape[1]
    tile_count = tiles.shape[0]
    user_count = user_emb.shape[0]
    user_blocks = user_count * lax.axis_size("ia") // tile_size
    item_blocks = item_emb.shape[0] * lax.axis_size("au") // tile_size
    live_mask = (jnp.arange(tile_count, dtype=jnp.int32) < live_tiles[0]).astype(jnp.float32)
    user_pick = (
        tile_user_block[None, :] == jnp.arange(user_blocks, dtype=jnp.int32)[:, None]
    ).astype(jnp.float32) * live_mask[None, :]
    item_pick = (
        tile_item_block[None, :] == jnp.arange(item_blocks, dtype=jnp.int32)[:, None]
    ).astype(jnp.float32) * live_mask[None, :]
    norm_user = lax.rsqrt(user_degree.astype(jnp.float32))[:, None]
    norm_item = lax.rsqrt(item_degree.astype(jnp.float32))[:, None]
    gathered_users = lax.all_gather(user_emb * norm_user, "ia", axis=0, tiled=True)
    users_now, items_now = (user_emb, item_emb)
    user_total, item_total = (user_emb, item_emb)
    for layer_index in range(LAYERS):
        gathered_items = lax.all_gather(items_now * norm_item, "au", axis=0, tiled=True)
        toward_picked = gathered_items.reshape(item_blocks, tile_size, emb_width)[tile_item_block]
        toward_products = jnp.einsum(
            "tuk,tkd->tud", tiles, toward_picked, precision=lax.Precision.HIGHEST
        )
        toward_summed = jnp.dot(
            user_pick, toward_products.reshape(tile_count, -1), precision=lax.Precision.HIGHEST
        )
        partial_users = toward_summed.reshape(user_blocks * tile_size, emb_width)
        picked = gathered_users.reshape(user_blocks, tile_size, emb_width)[tile_user_block]
        products = jnp.einsum("tuk,tud->tkd", tiles, picked, precision=lax.Precision.HIGHEST)
        summed = jnp.dot(
            item_pick, products.reshape(tile_count, -1), precision=lax.Precision.HIGHEST
        )
        partial_items = summed.reshape(item_blocks * tile_size, emb_width)
        users_now = (
            lax.psum_scatter(partial_users, "ia", scatter_dimension=0, tiled=True) * norm_user
        )
        if layer_index + 1 < LAYERS:
            gathered_users = lax.all_gather(users_now * norm_user, "ia", axis=0, tiled=True)
        items_now = (
            lax.psum_scatter(partial_items, "au", scatter_dimension=0, tiled=True) * norm_item
        )
        user_total = user_total + users_now
        item_total = item_total + items_now
    return (user_total / (LAYERS + 1.0), item_total / (LAYERS + 1.0))


def solution(mesh):
    in_specs = (
        P(("au", "ia"), None),
        P(("ia", "au"), None),
        P(("au", "ia")),
        P(("ia", "au")),
        P(("au", "ia"), None, None),
        P(("au", "ia")),
        P(("au", "ia")),
        P(("au", "ia")),
    )
    out_specs = (P(("au", "ia"), None), P(("ia", "au"), None))
    return jax.shard_map(
        per_device, mesh=mesh, in_specs=in_specs, out_specs=out_specs, check_vma=False
    )
```

profile of v0, /device:TPU:2, one launch (start us, length us, event | category | flops | bytes accessed | tf_op | source)
XLA Modules:
  0.0 559.2 jit_solution(12804511916847766787)
XLA Ops:
  11.1 43.4 %all-gather.7.cloned.1.call-done = f32[4096,128]{1,0:T(8,128)} async-done(((f32[512,128]{1,0:T(8,128)}), f32[4096,128]{1,0:T(8,128)}) %all-gather.7.cloned.1.call-update) | async-done | bytes 2097168 | tf_op jit(solution)/shard_map/all_gather | solution.py:34
  54.5 5.9 %gather_fusion.1 = f32[128,128,128]{2,1,0:T(8,128)} fusion(f32[32,128,128]{2,1,0:T(8,128)} %bitcast.32, s32[1024]{0:T(1024)S(1)} %pad_clamp_fusion), kind=kCustom, calls=%fused_computation.1 | custom fusion | bytes 16777728 | tf_op jit(solution)/shard_map/gather | solution.py:47
  60.4 19.0 %convolution_bitcast_fusion.2 = f32[128,128,128]{1,2,0:T(8,128)} fusion(f32[128,128,128]{2,1,0:T(8,128)} %gather_fusion.1, f32[128,128,128]{2,1,0:T(8,128)} %param.12), kind=kOutput, calls=%fused_computation.6 | convolution fusion | flops 3221225472 | bytes 25165824 | tf_op jit(solution)/shard_map/tuk,tud->tkd/dot_general | solution.py:48
  79.4 9.4 %copy.13 = f32[128,128,128]{0,2,1:T(8,128)} copy(f32[128,128,128]{1,2,0:T(8,128)} %convolution_bitcast_fusion.2) | data formatting | bytes 16777216 | tf_op jit(solution)/shard_map/tuk,tud->tkd/dot_general | solution.py:48
  88.8 10.8 %fusion.2 = f32[32,16384]{1,0:T(8,128)S(1)} fusion(f32[128,16384]{0,1:T(8,128)} %bitcast.35, s32[128]{0:T(128)S(1)} %copy-done.4, f32[128]{0:T(128)S(1)} %compare_convert_fusion), kind=kOutput, calls=%fused_computation.16 | convolution fusion | flops 805314560 | bytes 10486784 | tf_op jit(solution)/shard_map/dot_general | solution.py:49
  101.2 84.7 %reduce-scatter.7.cloned.1.call-done = f32[128,128]{1,0:T(8,128)} async-done(((f32[4096,128]{1,0:T(8,128)}), f32[128,128]{1,0:T(8,128)}) %reduce-scatter.7.cloned.1.call-update) | async-done | bytes 65552 | tf_op jit(solution)/shard_map/reduce_scatter | solution.py:59
  188.6 48.6 %all-gather.9.cloned.1.call-done = f32[4096,128]{1,0:T(8,128)} async-done(((f32[128,128]{1,0:T(8,128)}), f32[4096,128]{1,0:T(8,128)}) %all-gather.9.cloned.1.call-update) | async-done | bytes 2097168 | tf_op jit(solution)/shard_map/all_gather | solution.py:38
  237.2 5.9 %gather_fusion.2 = f32[128,128,128]{2,1,0:T(8,128)} fusion(f32[32,128,128]{2,1,0:T(8,128)} %bitcast.31, s32[1024]{0:T(1024)S(1)} %pad_clamp_fusion.1), kind=kCustom, calls=%fused_computation.2 | custom fusion | bytes 16777728 | tf_op jit(solution)/shard_map/gather | solution.py:39
  243.1 19.0 %convolution_bitcast_fusion.1 = f32[128,128,128]{1,2,0:T(8,128)} fusion(f32[128,128,128]{2,1,0:T(8,128)} %gather_fusion.2, f32[128,128,128]{2,1,0:T(8,128)} %param.12), kind=kOutput, calls=%fused_computation.5 | convolution fusion | flops 3221225472 | bytes 25165824 | tf_op jit(solution)/shard_map/tuk,tkd->tud/dot_general | solution.py:40
  262.1 9.4 %copy.15 = f32[128,128,128]{0,2,1:T(8,128)} copy(f32[128,128,128]{1,2,0:T(8,128)} %convolution_bitcast_fusion.1) | data formatting | bytes 16777216 | tf_op jit(solution)/shard_map/tuk,tkd->tud/dot_general | solution.py:40
  271.6 10.7 %fusion.4 = f32[32,16384]{1,0:T(8,128)S(1)} fusion(f32[128,16384]{0,1:T(8,128)} %bitcast.36, f32[128]{0:T(128)S(1)} %compare_convert_fusion, s32[128]{0:T(128)S(1)} %copy-done.3), kind=kOutput, calls=%fused_computation.18 | convolution fusion | flops 805314560 | bytes 10486784 | tf_op jit(solution)/shard_map/dot_general | solution.py:43
  284.1 4.3 all-gather.5.cloned.1.call-done
  288.4 5.9 %gather_fusion = f32[128,128,128]{2,1,0:T(8,128)} fusion(f32[32,128,128]{2,1,0:T(8,128)} %bitcast.30, s32[1024]{0:T(1024)S(1)} %pad_clamp_fusion.1), kind=kCustom, calls=%fused_computation | custom fusion | bytes 16777728 | tf_op jit(solution)/shard_map/gather | solution.py:39
  294.3 19.0 %convolution_bitcast_fusion.3 = f32[128,128,128]{1,2,0:T(8,128)} fusion(f32[128,128,128]{2,1,0:T(8,128)} %gather_fusion, f32[128,128,128]{2,1,0:T(8,128)} %param.12), kind=kOutput, calls=%fused_computation.7 | convolution fusion | flops 3221225472 | bytes 25165824 | tf_op jit(solution)/shard_map/tuk,tkd->tud/dot_general | solution.py:40
  313.3 9.5 %copy.11 = f32[128,128,128]{0,2,1:T(8,128)} copy(f32[128,128,128]{1,2,0:T(8,128)} %convolution_bitcast_fusion.3) | data formatting | bytes 16777216 | tf_op jit(solution)/shard_map/tuk,tkd->tud/dot_general | solution.py:40
  322.7 10.8 %fusion.6 = f32[32,16384]{1,0:T(8,128)S(1)} fusion(f32[128,16384]{0,1:T(8,128)} %bitcast.37, f32[128]{0:T(128)S(1)} %compare_convert_fusion, s32[128]{0:T(128)S(1)} %copy-done.3), kind=kOutput, calls=%fused_computation.20 | convolution fusion | flops 805314560 | bytes 10486784 | tf_op jit(solution)/shard_map/dot_general | solution.py:43
  335.2 41.9 %reduce-scatter.5.cloned.1.call-done = f32[512,128]{1,0:T(8,128)} async-done(((f32[4096,128]{1,0:T(8,128)}), f32[512,128]{1,0:T(8,128)}) %reduce-scatter.5.cloned.1.call-update) | async-done | bytes 262160 | tf_op jit(solution)/shard_map/reduce_scatter | solution.py:54
  377.1 2.0 multiply_multiply_fusion
  379.3 39.8 %all-gather.11.cloned.1.call-done = f32[4096,128]{1,0:T(8,128)} async-done(((f32[512,128]{1,0:T(8,128)}), f32[4096,128]{1,0:T(8,128)}) %all-gather.11.cloned.1.call-update) | async-done | bytes 2097168 | tf_op jit(solution)/shard_map/all_gather | solution.py:57
  419.2 5.9 %gather_fusion.3 = f32[128,128,128]{2,1,0:T(8,128)} fusion(f32[32,128,128]{2,1,0:T(8,128)} %bitcast.33, s32[1024]{0:T(1024)S(1)} %pad_clamp_fusion), kind=kCustom, calls=%fused_computation.3 | custom fusion | bytes 16777728 | tf_op jit(solution)/shard_map/gather | solution.py:47
  425.1 19.0 %convolution_bitcast_fusion = f32[128,128,128]{1,2,0:T(8,128)} fusion(f32[128,128,128]{2,1,0:T(8,128)} %gather_fusion.3, f32[128,128,128]{2,1,0:T(8,128)} %param.12), kind=kOutput, calls=%fused_computation.4 | convolution fusion | flops 3221225472 | bytes 25165824 | tf_op jit(solution)/shard_map/tuk,tud->tkd/dot_general | solution.py:48
  444.1 9.4 %copy.17 = f32[128,128,128]{0,2,1:T(8,128)} copy(f32[128,128,128]{1,2,0:T(8,128)} %convolution_bitcast_fusion) | data formatting | bytes 16777216 | tf_op jit(solution)/shard_map/tuk,tud->tkd/dot_general | solution.py:48
  453.5 10.7 %fusion = f32[32,16384]{1,0:T(8,128)S(1)} fusion(f32[128,16384]{0,1:T(8,128)} %bitcast.34, s32[128]{0:T(128)S(1)} %copy-done.4, f32[128]{0:T(128)S(1)} %compare_convert_fusion), kind=kOutput, calls=%fused_computation.14 | convolution fusion | flops 805314560 | bytes 10486784 | tf_op jit(solution)/shard_map/dot_general | solution.py:49
  465.8 84.8 %reduce-scatter.11.cloned.1.call-done = f32[128,128]{1,0:T(8,128)} async-done(((f32[4096,128]{1,0:T(8,128)}), f32[128,128]{1,0:T(8,128)}) %reduce-scatter.11.cloned.1.call-update) | async-done | bytes 65552 | tf_op jit(solution)/shard_map/reduce_scatter | solution.py:59
  (43 shorter events, 14.2 us)
Async XLA Ops:
  7.2 47.3 %all-gather.7.cloned.1.call-start = ((), (), s32[]{:S(2)}) async-start(), calls=%async_computation.6 | async-start | bytes 2359296 | tf_op jit(solution)/shard_map/all_gather | solution.py:34
  9.7 176.2 %reduce-scatter.7.cloned.1.call-start = ((), (), s32[]{:S(2)}) async-start(), calls=%async_computation.7 | async-start | bytes 2162688 | tf_op jit(solution)/shard_map/reduce_scatter | solution.py:59
  79.4 9.4 %copy-start.4 = (s32[128]{0:T(128)S(1)}, s32[128]{0:T(128)}, u32[]{:S(2)}) copy-start(s32[128]{0:T(128)} %param.14) | copy-start | bytes 1540
  88.8 12.4 %copy-start.5 = (s32[128]{0:T(128)S(1)}, s32[128]{0:T(128)}, u32[]{:S(2)}) copy-start(s32[128]{0:T(128)} %param.11) | copy-start | bytes 1540
  88.8 97.1 %copy-start.1 = (f32[128,128]{1,0:T(8,128)S(1)}, f32[128,128]{1,0:T(8,128)}, u32[]{:S(2)}) copy-start(f32[128,128]{1,0:T(8,128)} %param.9) | copy-start | bytes 196612
  101.1 136.1 %all-gather.9.cloned.1.call-start = ((), (), s32[]{:S(2)}) async-start(), calls=%async_computation.8 | async-start | bytes 2162688 | tf_op jit(solution)/shard_map/all_gather | solution.py:38
  187.5 100.9 %all-gather.5.cloned.1.call-start = ((), (), s32[]{:S(2)}) async-start(), calls=%async_computation.4 | async-start | bytes 2162688 | tf_op jit(solution)/shard_map/all_gather | solution.py:38
  188.1 147.1 %reduce-scatter.9.cloned.1.call-start = ((), (), s32[]{:S(2)}) async-start(), calls=%async_computation.9 | async-start | bytes 2359296 | tf_op jit(solution)/shard_map/reduce_scatter | solution.py:54
  262.1 9.4 %copy-start.3 = (s32[128]{0:T(128)S(1)}, s32[128]{0:T(128)}, u32[]{:S(2)}) copy-start(s32[128]{0:T(128)} %param.13) | copy-start | bytes 1540
  283.8 93.2 %reduce-scatter.5.cloned.1.call-start = ((), (), s32[]{:S(2)}) async-start(), calls=%async_computation.5 | async-start | bytes 2359296 | tf_op jit(solution)/shard_map/reduce_scatter | solution.py:54
  322.7 54.4 %copy-start = (f32[512,128]{1,0:T(8,128)S(1)}, f32[512,128]{1,0:T(8,128)}, u32[]{:S(2)}) copy-start(f32[512,128]{1,0:T(8,128)} %param.8) | copy-start | bytes 786436
  335.1 84.1 %all-gather.11.cloned.1.call-start = ((), (), s32[]{:S(2)}) async-start(), calls=%async_computation.10 | async-start | bytes 2359296 | tf_op jit(solution)/shard_map/all_gather | solution.py:57
  379.1 171.6 %reduce-scatter.11.cloned.1.call-start = ((), (), s32[]{:S(2)}) async-start(), calls=%async_computation.11 | async-start | bytes 2162688 | tf_op jit(solution)/shard_map/reduce_scatter | solution.py:59
  453.5 97.1 %copy-start.2 = (f32[128,128]{1,0:T(8,128)S(1)}, f32[128,128]{1,0:T(8,128)}, u32[]{:S(2)}) copy-start(f32[128,128]{1,0:T(8,128)} %reduce-scatter.7.cloned.1.call-done) | copy-start | bytes 196612
Sparse Core Ops, SparseCore 0:
  10.4 44.0 all-gather.6
  101.2 84.6 reduce-scatter.6
  189.0 48.1 all-gather.8
  240.2 48.1 all-gather.4
  290.8 41.5 reduce-scatter.8
  335.2 41.8 reduce-scatter.4
  379.2 39.9 all-gather.10
  465.9 84.6 reduce-scatter.10
where the time goes:
time: 569 us; the launch traced here: 559 us
  waiting for transfers between devices  348 us (61%)
  matrix products  119 us (21%)
  local copies, waits for them, and re-layouts  67.5 us (12%)
  between operations  15.1 us (3%)
  other arithmetic  8.25 us (1%)
    reduce_scatter x2, waiting for transfers between devices, per_device(): lax.psum_scatter(partial_items, 'au', scatter_dimension=0, tiled=True)  170 us
    all_gather x2, waiting for transfers between devices, per_device(): lax.all_gather(items_now * norm_item, 'au', axis=0, tiled=True)  52.9 us
    all_gather x1, waiting for transfers between devices, per_device(): lax.all_gather(user_emb * norm_user, 'ia', axis=0, tiled=True)  43.4 us
    reduce_scatter x2, waiting for transfers between devices, per_device(): lax.psum_scatter(partial_users, 'ia', scatter_dimension=0, tiled=True)  41.9 us
    all_gather x1, waiting for transfers between devices, per_device(): lax.all_gather(users_now * norm_user, 'ia', axis=0, tiled=True)  39.8 us
    dot_general x2, matrix products, per_device(): jnp.einsum('tuk,tud->tkd', tiles, picked, precision=lax.Precision.HIGHEST)  38 us
    dot_general x2, matrix products, per_device(): jnp.einsum('tuk,tkd->tud', tiles, toward_picked, precision=lax.Precision....  38 us
    dot_general x2, matrix products, per_device(): jnp.dot(user_pick, toward_products.reshape(tile_count, -1), precision=lax...  21.5 us
  transfers between devices with their start and end apart: 8, of which 7 were waited for; matrix products, arithmetic and copies ran while one was open for 17% of the time, Pallas kernels for 0%

commit v1 on v0

--- a/solution.py
+++ b/solution.py
@@ -31,7 +31,9 @@
     ).astype(jnp.float32) * live_mask[None, :]
     norm_user = lax.rsqrt(user_degree.astype(jnp.float32))[:, None]
     norm_item = lax.rsqrt(item_degree.astype(jnp.float32))[:, None]
-    gathered_users = lax.all_gather(user_emb * norm_user, "ia", axis=0, tiled=True)
+    x_part = user_emb * norm_user
+    frame_out = lax.all_to_all(jnp.stack([x_part for _ in range(lax.psum(1, "ia"))]), "ia", 0, 0)
+    gathered_users = jnp.concatenate(frame_out, 0)
     users_now, items_now = (user_emb, item_emb)
     user_total, item_total = (user_emb, item_emb)
     for layer_index in range(LAYERS):

time: 569 us -> 581 us (1.021)
  starting transfers between devices: 1.18 us -> 9.6 us
    all_to_all x0 -> x1, waiting for transfers between devices: none -> 49.8 us  [per_device(): lax.all_to_all(jnp.stack([x_part for _ in range(lax.psum(1, 'ia'))]), 'ia...]
    all_gather x1 -> x0, waiting for transfers between devices: 43.4 us -> none  [per_device(): lax.all_gather(user_emb * norm_user, 'ia', axis=0, tiled=True)]
    all_to_all x0 -> x1, starting transfers between devices: none -> 8.47 us  [per_device(): lax.all_to_all(jnp.stack([x_part for _ in range(lax.psum(1, 'ia'))]), 'ia...]
  transfers between devices with their start and end apart: 8 -> 8, of which waited for: 7 -> 7; matrix products, arithmetic and copies ran while one was open for 17% -> 16% of each run, Pallas kernels for 0% -> 0%
where the time goes in v1:
time: 581 us; the launch traced here: 571 us
  waiting for transfers between devices  353 us (61%)
  matrix products  119 us (20%)
  local copies, waits for them, and re-layouts  67.2 us (12%)
  between operations  15.3 us (3%)
  starting transfers between devices  9.6 us (2%)
  other arithmetic  7.54 us (1%)
    reduce_scatter x2, waiting for transfers between devices, per_device(): lax.psum_scatter(partial_items, 'au', scatter_dimension=0, tiled=True)  167 us
    all_gather x2, waiting for transfers between devices, per_device(): lax.all_gather(items_now * norm_item, 'au', axis=0, tiled=True)  52.9 us
    all_to_all x1, waiting for transfers between devices, per_device(): lax.all_to_all(jnp.stack([x_part for _ in range(lax.psum(1, 'ia'))]), 'ia...  49.8 us
    reduce_scatter x2, waiting for transfers between devices, per_device(): lax.psum_scatter(partial_users, 'ia', scatter_dimension=0, tiled=True)  42 us
    all_gather x1, waiting for transfers between devices, per_device(): lax.all_gather(users_now * norm_user, 'ia', axis=0, tiled=True)  39.8 us
    dot_general x2, matrix products, per_device(): jnp.einsum('tuk,tud->tkd', tiles, picked, precision=lax.Precision.HIGHEST)  38 us
    dot_general x2, matrix products, per_device(): jnp.einsum('tuk,tkd->tud', tiles, toward_picked, precision=lax.Precision....  38 us
    dot_general x2, matrix products, per_device(): jnp.dot(user_pick, toward_products.reshape(tile_count, -1), precision=lax...  21.5 us
  transfers between devices with their start and end apart: 8, of which 7 were waited for; matrix products, arithmetic and copies ran while one was open for 16% of the time, Pallas kernels for 0%

profile of v1, /device:TPU:2, one launch (start us, length us, event | category | flops | bytes accessed | tf_op | source)
XLA Modules:
  0.0 571.3 jit_solution(5379299357950344501)
XLA Ops:
  10.4 8.5 %all-to-all-start = ((f32[8,512,128]{2,1,0:T(8,128)}), f32[8,512,128]{2,1,0:T(8,128)S(1)}, u32[]{:S(2)}, u32[]{:S(2)}) async-start(f32[8,512,128]{2,1,0:T(8,128)} %stack.2), calls=%async_computation.1 | async-start | bytes 4194304 | tf_op jit(solution)/shard_map/all_to_all | solution.py:35
  20.3 49.8 %all-to-all-done = f32[8,512,128]{2,1,0:T(8,128)S(1)} async-done(((f32[8,512,128]{2,1,0:T(8,128)}), f32[8,512,128]{2,1,0:T(8,128)S(1)}, u32[]{:S(2)}, u32[]{:S(2)}) %all-to-all-start) | async-done | bytes 2097184 | tf_op jit(solution)/shard_map/all_to_all | solution.py:35
  70.1 4.3 gather_fusion.1
  74.4 19.1 %convolution_bitcast_fusion.2 = f32[128,128,128]{1,2,0:T(8,128)} fusion(f32[128,128,128]{2,1,0:T(8,128)} %gather_fusion.1, f32[128,128,128]{2,1,0:T(8,128)} %param.12), kind=kOutput, calls=%fused_computation.6 | convolution fusion | flops 3221225472 | bytes 25165824 | tf_op jit(solution)/shard_map/tuk,tud->tkd/dot_general | solution.py:50
  93.5 9.4 %copy.13 = f32[128,128,128]{0,2,1:T(8,128)} copy(f32[128,128,128]{1,2,0:T(8,128)} %convolution_bitcast_fusion.2) | data formatting | bytes 16777216 | tf_op jit(solution)/shard_map/tuk,tud->tkd/dot_general | solution.py:50
  102.8 10.8 %fusion.2 = f32[32,16384]{1,0:T(8,128)S(1)} fusion(f32[128,16384]{0,1:T(8,128)} %bitcast.35, s32[128]{0:T(128)S(1)} %copy-done.4, f32[128]{0:T(128)S(1)} %compare_convert_fusion), kind=kOutput, calls=%fused_computation.16 | convolution fusion | flops 805314560 | bytes 10486784 | tf_op jit(solution)/shard_map/dot_general | solution.py:51
  115.2 82.5 %reduce-scatter.7.cloned.1.call-done = f32[128,128]{1,0:T(8,128)} async-done(((f32[4096,128]{1,0:T(8,128)}), f32[128,128]{1,0:T(8,128)}) %reduce-scatter.7.cloned.1.call-update) | async-done | bytes 65552 | tf_op jit(solution)/shard_map/reduce_scatter | solution.py:61
  200.6 48.4 %all-gather.6.cloned.1.call-done = f32[4096,128]{1,0:T(8,128)} async-done(((f32[128,128]{1,0:T(8,128)}), f32[4096,128]{1,0:T(8,128)}) %all-gather.6.cloned.1.call-update) | async-done | bytes 2097168 | tf_op jit(solution)/shard_map/all_gather | solution.py:40
  249.0 5.9 %gather_fusion.2 = f32[128,128,128]{2,1,0:T(8,128)} fusion(f32[32,128,128]{2,1,0:T(8,128)} %bitcast.32, s32[1024]{0:T(1024)S(1)} %pad_clamp_fusion.1), kind=kCustom, calls=%fused_computation.2 | custom fusion | bytes 16777728 | tf_op jit(solution)/shard_map/gather | solution.py:41
  255.0 19.0 %convolution_bitcast_fusion.1 = f32[128,128,128]{1,2,0:T(8,128)} fusion(f32[128,128,128]{2,1,0:T(8,128)} %gather_fusion.2, f32[128,128,128]{2,1,0:T(8,128)} %param.12), kind=kOutput, calls=%fused_computation.5 | convolution fusion | flops 3221225472 | bytes 25165824 | tf_op jit(solution)/shard_map/tuk,tkd->tud/dot_general | solution.py:42
  273.9 9.4 %copy.15 = f32[128,128,128]{0,2,1:T(8,128)} copy(f32[128,128,128]{1,2,0:T(8,128)} %convolution_bitcast_fusion.1) | data formatting | bytes 16777216 | tf_op jit(solution)/shard_map/tuk,tkd->tud/dot_general | solution.py:42
  283.4 10.7 %fusion.4 = f32[32,16384]{1,0:T(8,128)S(1)} fusion(f32[128,16384]{0,1:T(8,128)} %bitcast.36, f32[128]{0:T(128)S(1)} %compare_convert_fusion, s32[128]{0:T(128)S(1)} %copy-done.3), kind=kOutput, calls=%fused_computation.18 | convolution fusion | flops 805314560 | bytes 10486784 | tf_op jit(solution)/shard_map/dot_general | solution.py:45
  295.8 4.5 all-gather.4.cloned.1.call-done
  300.3 5.9 %gather_fusion = f32[128,128,128]{2,1,0:T(8,128)} fusion(f32[32,128,128]{2,1,0:T(8,128)} %bitcast.31, s32[1024]{0:T(1024)S(1)} %pad_clamp_fusion.1), kind=kCustom, calls=%fused_computation | custom fusion | bytes 16777728 | tf_op jit(solution)/shard_map/gather | solution.py:41
  306.3 19.0 %convolution_bitcast_fusion.3 = f32[128,128,128]{1,2,0:T(8,128)} fusion(f32[128,128,128]{2,1,0:T(8,128)} %gather_fusion, f32[128,128,128]{2,1,0:T(8,128)} %param.12), kind=kOutput, calls=%fused_computation.7 | convolution fusion | flops 3221225472 | bytes 25165824 | tf_op jit(solution)/shard_map/tuk,tkd->tud/dot_general | solution.py:42
  325.2 9.4 %copy.11 = f32[128,128,128]{0,2,1:T(8,128)} copy(f32[128,128,128]{1,2,0:T(8,128)} %convolution_bitcast_fusion.3) | data formatting | bytes 16777216 | tf_op jit(solution)/shard_map/tuk,tkd->tud/dot_general | solution.py:42
  334.7 10.8 %fusion.6 = f32[32,16384]{1,0:T(8,128)S(1)} fusion(f32[128,16384]{0,1:T(8,128)} %bitcast.37, f32[128]{0:T(128)S(1)} %compare_convert_fusion, s32[128]{0:T(128)S(1)} %copy-done.3), kind=kOutput, calls=%fused_computation.20 | convolution fusion | flops 805314560 | bytes 10486784 | tf_op jit(solution)/shard_map/dot_general | solution.py:45
  347.1 42.0 %reduce-scatter.5.cloned.1.call-done = f32[512,128]{1,0:T(8,128)} async-done(((f32[4096,128]{1,0:T(8,128)}), f32[512,128]{1,0:T(8,128)}) %reduce-scatter.5.cloned.1.call-update) | async-done | bytes 262160 | tf_op jit(solution)/shard_map/reduce_scatter | solution.py:56
  391.3 39.8 %all-gather.8.cloned.1.call-done = f32[4096,128]{1,0:T(8,128)} async-done(((f32[512,128]{1,0:T(8,128)}), f32[4096,128]{1,0:T(8,128)}) %all-gather.8.cloned.1.call-update) | async-done | bytes 2097168 | tf_op jit(solution)/shard_map/all_gather | solution.py:59
  431.1 5.9 %gather_fusion.3 = f32[128,128,128]{2,1,0:T(8,128)} fusion(f32[32,128,128]{2,1,0:T(8,128)} %bitcast.33, s32[1024]{0:T(1024)S(1)} %pad_clamp_fusion), kind=kCustom, calls=%fused_computation.3 | custom fusion | bytes 16777728 | tf_op jit(solution)/shard_map/gather | solution.py:49
  437.0 19.0 %convolution_bitcast_fusion = f32[128,128,128]{1,2,0:T(8,128)} fusion(f32[128,128,128]{2,1,0:T(8,128)} %gather_fusion.3, f32[128,128,128]{2,1,0:T(8,128)} %param.12), kind=kOutput, calls=%fused_computation.4 | convolution fusion | flops 3221225472 | bytes 25165824 | tf_op jit(solution)/shard_map/tuk,tud->tkd/dot_general | solution.py:50
  456.0 9.4 %copy.17 = f32[128,128,128]{0,2,1:T(8,128)} copy(f32[128,128,128]{1,2,0:T(8,128)} %convolution_bitcast_fusion) | data formatting | bytes 16777216 | tf_op jit(solution)/shard_map/tuk,tud->tkd/dot_general | solution.py:50
  465.4 10.7 %fusion = f32[32,16384]{1,0:T(8,128)S(1)} fusion(f32[128,16384]{0,1:T(8,128)} %bitcast.34, s32[128]{0:T(128)S(1)} %copy-done.4, f32[128]{0:T(128)S(1)} %compare_convert_fusion), kind=kOutput, calls=%fused_computation.14 | convolution fusion | flops 805314560 | bytes 10486784 | tf_op jit(solution)/shard_map/dot_general | solution.py:51
  477.7 84.8 %reduce-scatter.11.cloned.1.call-done = f32[128,128]{1,0:T(8,128)} async-done(((f32[4096,128]{1,0:T(8,128)}), f32[128,128]{1,0:T(8,128)}) %reduce-scatter.11.cloned.1.call-update) | async-done | bytes 65552 | tf_op jit(solution)/shard_map/reduce_scatter | solution.py:61
  (43 shorter events, 17.0 us)
Async XLA Ops:
  10.4 59.7 %all-to-all-start = ((f32[8,512,128]{2,1,0:T(8,128)}), f32[8,512,128]{2,1,0:T(8,128)S(1)}, u32[]{:S(2)}, u32[]{:S(2)}) async-start(f32[8,512,128]{2,1,0:T(8,128)} %stack.2), calls=%async_computation.1 | async-start | bytes 4194304 | tf_op jit(solution)/shard_map/all_to_all | solution.py:35
  18.9 178.9 %reduce-scatter.7.cloned.1.call-start = ((), (), s32[]{:S(2)}) async-start(), calls=%async_computation.7 | async-start | bytes 2162688 | tf_op jit(solution)/shard_map/reduce_scatter | solution.py:61
  93.5 9.4 %copy-start.4 = (s32[128]{0:T(128)S(1)}, s32[128]{0:T(128)}, u32[]{:S(2)}) copy-start(s32[128]{0:T(128)} %param.14) | copy-start | bytes 1540
  102.8 12.4 %copy-start.5 = (s32[128]{0:T(128)S(1)}, s32[128]{0:T(128)}, u32[]{:S(2)}) copy-start(s32[128]{0:T(128)} %param.11) | copy-start | bytes 1540
  102.8 94.9 %copy-start.1 = (f32[128,128]{1,0:T(8,128)S(1)}, f32[128,128]{1,0:T(8,128)}, u32[]{:S(2)}) copy-start(f32[128,128]{1,0:T(8,128)} %param.9) | copy-start | bytes 196612
  115.1 133.9 %all-gather.6.cloned.1.call-start = ((), (), s32[]{:S(2)}) async-start(), calls=%async_computation.8 | async-start | bytes 2162688 | tf_op jit(solution)/shard_map/all_gather | solution.py:40
  199.3 101.0 %all-gather.4.cloned.1.call-start = ((), (), s32[]{:S(2)}) async-start(), calls=%async_computation.5 | async-start | bytes 2162688 | tf_op jit(solution)/shard_map/all_gather | solution.py:40
  200.1 147.0 %reduce-scatter.9.cloned.1.call-start = ((), (), s32[]{:S(2)}) async-start(), calls=%async_computation.9 | async-start | bytes 2359296 | tf_op jit(solution)/shard_map/reduce_scatter | solution.py:56
  273.9 9.4 %copy-start.3 = (s32[128]{0:T(128)S(1)}, s32[128]{0:T(128)}, u32[]{:S(2)}) copy-start(s32[128]{0:T(128)} %param.13) | copy-start | bytes 1540
  295.6 93.5 %reduce-scatter.5.cloned.1.call-start = ((), (), s32[]{:S(2)}) async-start(), calls=%async_computation.6 | async-start | bytes 2359296 | tf_op jit(solution)/shard_map/reduce_scatter | solution.py:56
  334.7 54.4 %copy-start = (f32[512,128]{1,0:T(8,128)S(1)}, f32[512,128]{1,0:T(8,128)}, u32[]{:S(2)}) copy-start(f32[512,128]{1,0:T(8,128)} %param.8) | copy-start | bytes 786436
  347.0 84.1 %all-gather.8.cloned.1.call-start = ((), (), s32[]{:S(2)}) async-start(), calls=%async_computation.10 | async-start | bytes 2359296 | tf_op jit(solution)/shard_map/all_gather | solution.py:59
  391.1 171.5 %reduce-scatter.11.cloned.1.call-start = ((), (), s32[]{:S(2)}) async-start(), calls=%async_computation.11 | async-start | bytes 2162688 | tf_op jit(solution)/shard_map/reduce_scatter | solution.py:61
  465.4 97.1 %copy-start.2 = (f32[128,128]{1,0:T(8,128)S(1)}, f32[128,128]{1,0:T(8,128)}, u32[]{:S(2)}) copy-start(f32[128,128]{1,0:T(8,128)} %reduce-scatter.7.cloned.1.call-done) | copy-start | bytes 196612
Sparse Core Ops, SparseCore 0:
  115.3 82.4 reduce-scatter.6
  200.9 48.1 all-gather.5
  252.2 48.1 all-gather.3
  302.7 41.5 reduce-scatter.8
  347.1 41.8 reduce-scatter.4
  391.2 39.8 all-gather.7
  477.8 84.6 reduce-scatter.10
